TPU v7x, 512 devices: a whole 4x4x16 slice. The times are simulated.
512 devices in a mesh: dp: 16 (over z), pipe: 4 (over x), tensor: 8 (over y, core).
Axes of the slice: x: 4, y: 4, z: 16, core: 2. Of those that a mesh axis runs over, the one named last changes fastest.
Arguments:
- tokens: bfloat16 [16384, 8192], P('dp', ('pipe', 'tensor')), may hold values from -6 to 6
- key_value_weight: bfloat16 [8192, 2048], P(('pipe', 'tensor')), may hold values from -0.0625 to 0.0625
- adapter_down: bfloat16 [96, 8192, 128], P(None, ('pipe', 'tensor', 'dp')), may hold values from -0.0625 to 0.0625
- adapter_up: bfloat16 [96, 64, 2048], P(None, 'dp'), may hold values from -0.75 to 0.75
- tenant_of_block: int32 [128], replicated, may hold values from 0 to 95
- slot_of_tenant: int32 [96], replicated, may hold values from 0 to 95, each once
- cotangent: bfloat16 [16384, 2048], P(('dp', 'pipe', 'tensor')), may hold values from -1.5 to 1.5
Outputs:
- key_value: bfloat16 [16384, 2048], P(('dp', 'pipe', 'tensor'))
- input_grad: bfloat16 [16384, 8192], P('dp', ('pipe', 'tensor'))
- grad_a: float32 [96, 8192, 128], P(None, ('pipe', 'tensor', 'dp'))
- grad_b: float32 [96, 64, 2048], P(None, 'dp', ('pipe', 'tensor'))
Inputs may be any that keep to these rules, and one draw needn't show every extreme that they name: `slot_of_tenant`: each slot holds exactly one tenant.
All inputs are finite; a program needn't handle non-finite values.
Results may differ from a plain program's by a relative error of at most 0.017.
Values may be sent and summed in bfloat16 or wider, within the bound.
A program may use at most 64 MiB of HBM per device.

v0:
```python
import jax
import jax.numpy as jnp
from jax import lax
from jax.sharding import PartitionSpec as P

KEY_WIDTH = 1024
ADAPTER_RANK = 64
BLOCK = 128


def body(
    tokens, key_value_weight, adapter_down, adapter_up, tenant_of_block, slot_of_tenant, cotangent
):
    data_count = lax.axis_size("dp")
    group_count = lax.axis_size(("pipe", "tensor"))
    my_group = lax.axis_index(("pipe", "tensor"))
    tok_dev, feature_count = tokens.shape
    blocks_dev = tok_dev // BLOCK
    row_count = tok_dev // group_count
    tenant_list = slot_of_tenant.shape[0]
    all_blocks = tenant_of_block.shape[0]
    tenant_ids = lax.broadcasted_iota(jnp.int32, (all_blocks, tenant_list), 1)
    slot_of_block = jnp.sum(
        jnp.where(tenant_of_block[:, None] == tenant_ids, slot_of_tenant[None, :], 0), axis=1
    )
    slot_match = slot_of_block[:, None] == tenant_ids
    down_rows = adapter_down.shape[1]
    a_send = jnp.dot(
        slot_match.astype(jnp.bfloat16),
        adapter_down.reshape(tenant_list, down_rows * 2 * ADAPTER_RANK),
        preferred_element_type=jnp.float32,
    )
    a_send = a_send.astype(jnp.bfloat16).reshape(all_blocks, down_rows, 2 * ADAPTER_RANK)
    own_block = my_group * row_count // BLOCK
    own_slots = lax.dynamic_index_in_dim(
        slot_of_block.reshape(data_count, blocks_dev), own_block, 1, False
    )
    owner_choice = (
        own_slots[:, None] == lax.broadcasted_iota(jnp.int32, (data_count, tenant_list), 1)
    ).astype(jnp.bfloat16)
    up_rows = adapter_up.shape[1]
    b_send = jnp.dot(
        owner_choice,
        adapter_up.reshape(tenant_list, up_rows * 2 * KEY_WIDTH),
        preferred_element_type=jnp.float32,
    )
    b_send = b_send.astype(jnp.bfloat16).reshape(data_count, up_rows, 2 * KEY_WIDTH)
    down_blocks, b_own = (
        lax.all_to_all(a_send, "dp", split_axis=0, concat_axis=1, tiled=True),
        lax.all_to_all(b_send, "dp", split_axis=0, concat_axis=1, tiled=True),
    )
    b_own = b_own[0]
    tok_blocks = tokens.reshape(blocks_dev, BLOCK, feature_count)
    low_part = jnp.einsum(
        "bif,bfr->bir", tok_blocks, down_blocks, preferred_element_type=jnp.float32
    ).reshape(tok_dev, 2 * ADAPTER_RANK)
    low_all = lax.psum(low_part.astype(jnp.bfloat16), ("pipe", "tensor"))
    base_out = lax.psum_scatter(
        jnp.dot(tokens, key_value_weight, preferred_element_type=jnp.float32).astype(jnp.bfloat16),
        ("pipe", "tensor"),
        scatter_dimension=0,
        tiled=True,
    ).astype(jnp.float32)
    low_rows = lax.dynamic_slice_in_dim(low_all, my_group * row_count, row_count, 0)
    lowrank = jnp.concatenate(
        [
            jnp.dot(
                low_rows[:, :ADAPTER_RANK], b_own[:, :KEY_WIDTH], preferred_element_type=jnp.float32
            ),
            jnp.dot(
                low_rows[:, ADAPTER_RANK:], b_own[:, KEY_WIDTH:], preferred_element_type=jnp.float32
            ),
        ],
        axis=1,
    )
    key_value = (base_out + lowrank).astype(jnp.bfloat16)
    contract_last = (((1,), (1,)), ((), ()))
    grad_rows = jnp.concatenate(
        [
            lax.dot_general(
                cotangent[:, :KEY_WIDTH],
                b_own[:, :KEY_WIDTH],
                contract_last,
                preferred_element_type=jnp.float32,
            ),
            lax.dot_general(
                cotangent[:, KEY_WIDTH:],
                b_own[:, KEY_WIDTH:],
                contract_last,
                preferred_element_type=jnp.float32,
            ),
        ],
        axis=1,
    )
    grad_rows = grad_rows.astype(jnp.bfloat16)
    cot_all, grad_low = (
        lax.all_gather(cotangent, ("pipe", "tensor"), axis=0, tiled=True),
        lax.all_gather(grad_rows, ("pipe", "tensor"), axis=0, tiled=True),
    )
    grad_blocks = grad_low.reshape(blocks_dev, BLOCK, 2 * ADAPTER_RANK)
    input_grad = lax.dot_general(
        cot_all, key_value_weight, contract_last, preferred_element_type=jnp.float32
    )
    input_grad = input_grad + jnp.einsum(
        "bir,bfr->bif", grad_blocks, down_blocks, preferred_element_type=jnp.float32
    ).reshape(tok_dev, feature_count)
    input_grad = input_grad.astype(jnp.bfloat16)
    grad_a_part = jnp.einsum(
        "bif,bir->bfr", tok_blocks, grad_blocks, preferred_element_type=jnp.float32
    )
    col_count = 2 * KEY_WIDTH // group_count
    col_start = my_group * col_count
    half_index = col_start // KEY_WIDTH
    low_half = lax.dynamic_slice_in_dim(
        low_all, half_index * ADAPTER_RANK, ADAPTER_RANK, 1
    ).reshape(blocks_dev, BLOCK, ADAPTER_RANK)
    cot_cols = lax.dynamic_slice_in_dim(cot_all, col_start, col_count, 1).reshape(
        blocks_dev, BLOCK, col_count
    )
    grad_b_part = jnp.einsum("bir,bic->brc", low_half, cot_cols, preferred_element_type=jnp.float32)
    grad_a_recv, grad_b_recv = (
        lax.all_to_all(
            grad_a_part.astype(jnp.bfloat16), "dp", split_axis=1, concat_axis=0, tiled=True
        ).astype(grad_a_part.dtype),
        lax.all_to_all(
            grad_b_part.astype(jnp.bfloat16), "dp", split_axis=1, concat_axis=0, tiled=True
        ).astype(grad_b_part.dtype),
    )
    slot_weight = slot_match.astype(jnp.float32)
    grad_a = jnp.einsum(
        "bt,bx->tx",
        slot_weight,
        grad_a_recv.reshape(all_blocks, down_rows * 2 * ADAPTER_RANK),
        precision=lax.Precision.HIGHEST,
    )
    grad_a = grad_a.reshape(tenant_list, down_rows, 2 * ADAPTER_RANK)
    grad_b = jnp.einsum(
        "bt,bx->tx",
        slot_weight,
        grad_b_recv.reshape(all_blocks, grad_b_recv.shape[1] * col_count),
        precision=lax.Precision.HIGHEST,
    )
    grad_b = grad_b.reshape(tenant_list, grad_b_recv.shape[1], col_count)
    return (key_value, input_grad, grad_a, grad_b)


def solution(mesh):
    placed = (
        P("dp", ("pipe", "tensor")),
        P(("pipe", "tensor"), None),
        P(None, ("pipe", "tensor", "dp"), None),
        P(None, "dp", None),
        P(),
        P(),
        P(("dp", "pipe", "tensor"), None),
    )
    return jax.shard_map(
        body,
        mesh=mesh,
        in_specs=placed,
        out_specs=(
            P(("dp", "pipe", "tensor"), None),
            P("dp", ("pipe", "tensor")),
            P(None, ("pipe", "tensor", "dp"), None),
            P(None, "dp", ("pipe", "tensor")),
        ),
        check_vma=False,
    )
```

profile of v0, /device:TPU:2, one launch (start us, length us, event | category | flops | bytes accessed | tf_op | source)
XLA Modules:
  0.0 395.1 jit_solution(17106891758424243477)
XLA Ops:
  7.2 0.9 select_reduce_fusion
  8.1 1.3 fusion.2
  9.6 44.1 %all_to_all.57 = bf16[128,16,128]{2,1,0:T(8,128)(2,1)S(1)} all-to-all(bf16[128,16,128]{2,1,0:T(8,128)(2,1)S(1)} %bitcast.78), channel_id=1, replica_groups=mesh['dp'=16,'pipe'=4,'tensor'=8] {'dp'}, dimensions={0} | all-to-all | bytes 1048576 | tf_op jit(solution)/shard_map/all_to_all | solution.py:49
  53.7 0.8 copy-done.2
  54.8 0.9 copy.41
  55.7 3.2 convolution_convert_fusion.1
  59.8 2.4 copy.61
  63.0 24.5 %all_to_all.58 = bf16[16,4,2048]{2,1,0:T(4,128)(2,1)S(1)} all-to-all(bf16[16,4,2048]{2,1,0:T(4,128)(2,1)S(1)} %reshape.64), channel_id=1, replica_groups=mesh['dp'=16,'pipe'=4,'tensor'=8] {'dp'}, dimensions={0} | all-to-all | bytes 524288 | tf_op jit(solution)/shard_map/all_to_all | solution.py:50
  88.4 24.9 %all_gather.7 = bf16[1024,128]{1,0:T(8,128)(2,1)S(1)} all-gather(bf16[32,128]{1,0:T(8,128)(2,1)S(1)} %pad_maximum_fusion), channel_id=1, replica_groups=mesh['dp'=16,'pipe'=4,'tensor'=8] {'pipe','tensor'}, dimensions={0}, use_global_device_ids=true | all-gather | bytes 270336 | tf_op jit(solution)/shard_map/all_gather | solution.py:98
  113.6 1.1 copy.43
  114.7 5.8 %all-to-all-start.2 = ((bf16[8,256,128]{2,0,1:T(8,128)(2,1)}), bf16[8,256,128]{2,0,1:T(8,128)(2,1)S(1)}, u32[]{:S(2)}, u32[]{:S(2)}) async-start(bf16[8,256,128]{2,0,1:T(8,128)(2,1)} %copy.43), calls=%async_computation.3 | async-start | bytes 1048576 | tf_op jit(solution)/shard_map/all_to_all | solution.py:122
  120.8 63.9 %all-reduce.2.cloned.1.call-done = bf16[1024,128]{0,1:T(8,128)(2,1)} async-done(((bf16[1024,128]{0,1:T(8,128)(2,1)}), bf16[1024,128]{0,1:T(8,128)(2,1)}) %all-reduce.2.cloned.1.call-update) | async-done | bytes 262160 | tf_op jit(solution)/shard_map/psum | solution.py:57
  184.8 1.2 fusion.14
  185.9 1.2 fusion.11
  187.7 1.3 copy.53
  189.1 105.7 %reduce-scatter.2.cloned.1.call-done = bf16[32,2048]{1,0:T(8,128)(2,1)} async-done(((bf16[1024,2048]{1,0:T(8,128)(2,1)}), bf16[32,2048]{1,0:T(8,128)(2,1)}) %reduce-scatter.2.cloned.1.call-update) | async-done | bytes 131088 | tf_op jit(solution)/shard_map/reduce_scatter | solution.py:58
  294.8 1.6 fusion.7
  296.4 62.4 %all-gather.2.cloned.1.call-done = bf16[1024,2048]{1,0:T(8,128)(2,1)} async-done(((bf16[32,2048]{1,0:T(8,128)(2,1)}), bf16[1024,2048]{1,0:T(8,128)(2,1)}) %all-gather.2.cloned.1.call-update) | async-done | bytes 4194320 | tf_op jit(solution)/shard_map/all_gather | solution.py:97
  358.8 1.1 constant_dynamic-slice_fusion
  359.9 1.1 convolution_convert_fusion.5
  361.9 12.3 %all-to-all-start.3 = ((bf16[16,2,1024]{2,1,0:T(2,128)(2,1)}), bf16[16,2,1024]{2,1,0:T(2,128)(2,1)S(1)}, u32[]{:S(2)}, u32[]{:S(2)}) async-start(bf16[16,2,1024]{2,1,0:T(2,128)(2,1)} %reshape.73), calls=%async_computation.4 | async-start | bytes 131072 | tf_op jit(solution)/shard_map/all_to_all | solution.py:125
  374.2 4.3 %fusion = bf16[1024,256]{1,0:T(8,128)(2,1)} fusion(f32[1024,256]{1,0:T(8,128)S(1)} %bitcast.81, bf16[1024,2048]{1,0:T(8,128)(2,1)} %all-gather.2.cloned.1.call-done, bf16[256,2048]{1,0:T(8,128)(2,1)S(1)} %copy-done), kind=kOutput, calls=%fused_computation.4 | convolution fusion | flops 1074266112 | bytes 6815744 | tf_op jit(solution)/shard_map/dot_general | solution.py:101
  378.4 8.9 %all-to-all-done.3 = bf16[16,2,1024]{2,1,0:T(2,128)(2,1)S(1)} async-done(((bf16[16,2,1024]{2,1,0:T(2,128)(2,1)}), bf16[16,2,1024]{2,1,0:T(2,128)(2,1)S(1)}, u32[]{:S(2)}, u32[]{:S(2)}) %all-to-all-start.3) | async-done | bytes 65568 | tf_op jit(solution)/shard_map/all_to_all | solution.py:125
  387.8 0.8 fusion.19
  (39 shorter events, 5.5 us)
Async XLA Ops:
  7.2 48.6 %copy-start = (bf16[256,2048]{1,0:T(8,128)(2,1)S(1)}, bf16[256,2048]{1,0:T(8,128)(2,1)}, u32[]{:S(2)}) copy-start(bf16[256,2048]{1,0:T(8,128)(2,1)} %param.8) | copy-start | bytes 3145732
  7.2 47.3 %copy-start.1 = (bf16[1024,256]{1,0:T(8,128)(2,1)S(1)}, bf16[1024,256]{1,0:T(8,128)(2,1)}, u32[]{:S(2)}) copy-start(bf16[1024,256]{1,0:T(8,128)(2,1)} %param.7) | copy-start | bytes 1572868
  7.2 177.6 %all-reduce.2.cloned.1.call-start = ((), (), s32[]{:S(2)}) async-start(), calls=%async_computation.6 | async-start | bytes 524288 | tf_op jit(solution)/shard_map/psum | solution.py:57
  53.7 0.8 copy-start.2
  55.7 239.1 %reduce-scatter.2.cloned.1.call-start = ((), (), s32[]{:S(2)}) async-start(), calls=%async_computation.5 | async-start | bytes 4325376 | tf_op jit(solution)/shard_map/reduce_scatter | solution.py:58
  59.0 28.6 %copy-start.5 = (bf16[32,2048]{1,0:T(8,128)(2,1)S(1)}, bf16[32,2048]{1,0:T(8,128)(2,1)}, u32[]{:S(2)}) copy-start(bf16[32,2048]{1,0:T(8,128)(2,1)} %param.13) | copy-start | bytes 393220
  59.0 299.8 %all-gather.2.cloned.1.call-start = ((), (), s32[]{:S(2)}) async-start(), calls=%async_computation.7 | async-start | bytes 4325376 | tf_op jit(solution)/shard_map/all_gather | solution.py:97
  62.8 57.7 %copy-start.3 = (bf16[16,8,16,128]{3,2,0,1:T(8,128)(2,1)S(1)}, bf16[16,8,16,128]{3,2,0,1:T(8,128)(2,1)}, u32[]{:S(2)}) copy-start(bf16[16,8,16,128]{3,2,0,1:T(8,128)(2,1)} %copy-done.2) | copy-start | bytes 1572868
  87.6 0.7 copy-start.4
  114.7 72.4 %all-to-all-start.2 = ((bf16[8,256,128]{2,0,1:T(8,128)(2,1)}), bf16[8,256,128]{2,0,1:T(8,128)(2,1)S(1)}, u32[]{:S(2)}, u32[]{:S(2)}) async-start(bf16[8,256,128]{2,0,1:T(8,128)(2,1)} %copy.43), calls=%async_computation.3 | async-start | bytes 1048576 | tf_op jit(solution)/shard_map/all_to_all | solution.py:122
  361.9 25.5 %all-to-all-start.3 = ((bf16[16,2,1024]{2,1,0:T(2,128)(2,1)}), bf16[16,2,1024]{2,1,0:T(2,128)(2,1)S(1)}, u32[]{:S(2)}, u32[]{:S(2)}) async-start(bf16[16,2,1024]{2,1,0:T(2,128)(2,1)} %reshape.73), calls=%async_computation.4 | async-start | bytes 131072 | tf_op jit(solution)/shard_map/all_to_all | solution.py:125
Sparse Core Ops, SparseCore 0:
  55.8 128.9 all-reduce.1
  189.3 105.4 reduce-scatter.1
  297.9 60.8 all-gather.1
where the time goes:
time: 396 us; the launch traced here: 395 us
  waiting for transfers between devices  242 us (61%)
  blocking collectives  93.4 us (24%)
  starting transfers between devices  18.2 us (5%)
  matrix products  15 us (4%)
  between operations  14 us (4%)
  local copies, waits for them, and re-layouts  10.2 us (3%)
    reduce_scatter x1, waiting for transfers between devices, body(): lax.psum_scatter(jnp.dot(tokens, key_value_weight, preferred_element_type...  106 us
    psum x1, waiting for transfers between devices, body(): low_all = lax.psum(low_part.astype(jnp.bfloat16), ('pipe', 'tensor'))  63.9 us
    all_gather x1, waiting for transfers between devices, body(): lax.all_gather(cotangent, ('pipe', 'tensor'), axis=0, tiled=True)  62.4 us
    all_to_all x1, blocking collectives, body(): lax.all_to_all(a_send, 'dp', split_axis=0, concat_axis=1, tiled=True)  44.1 us
    all_gather x1, blocking collectives, body(): lax.all_gather(grad_rows, ('pipe', 'tensor'), axis=0, tiled=True)  24.9 us
    all_to_all x1, blocking collectives, body(): lax.all_to_all(b_send, 'dp', split_axis=0, concat_axis=1, tiled=True)  24.5 us
    all_to_all x1, starting transfers between devices, body(): lax.all_to_all(grad_b_part.astype(jnp.bfloat16), 'dp', split_axis=1, conc...  12.3 us
    all_to_all x1, waiting for transfers between devices, body(): lax.all_to_all(grad_b_part.astype(jnp.bfloat16), 'dp', split_axis=1, conc...  8.89 us
  transfers between devices with their start and end apart: 5, of which 4 were waited for; matrix products, arithmetic and copies ran while one was open for 5% of the time, Pallas kernels for 0%

commit v1 on v0

--- a/solution.py
+++ b/solution.py
@@ -2,6 +2,7 @@
 import jax.numpy as jnp
 from jax import lax
 from jax.sharding import PartitionSpec as P
+from jax.lax import psum
 
 KEY_WIDTH = 1024
 ADAPTER_RANK = 64
@@ -54,7 +55,7 @@
     low_part = jnp.einsum(
         "bif,bfr->bir", tok_blocks, down_blocks, preferred_element_type=jnp.float32
     ).reshape(tok_dev, 2 * ADAPTER_RANK)
-    low_all = lax.psum(low_part.astype(jnp.bfloat16), ("pipe", "tensor"))
+    low_all = psum(psum(low_part.astype(jnp.bfloat16), axis_name="tensor"), axis_name="pipe")
     base_out = lax.psum_scatter(
         jnp.dot(tokens, key_value_weight, preferred_element_type=jnp.float32).astype(jnp.bfloat16),
         ("pipe", "tensor"),

time: 396 us -> 339 us (0.86)
  waiting for transfers between devices: 242 us -> 179 us
  blocking collectives: 93.4 us -> 97.4 us
    reduce_scatter x1, waiting for transfers between devices: 106 us -> 9.04 us  [body(): lax.psum_scatter(jnp.dot(tokens, key_value_weight, preferred_element_type...]
    all_to_all x1, waiting for transfers between devices: 0.01 us -> 26.6 us  [body(): lax.all_to_all(grad_a_part.astype(jnp.bfloat16), 'dp', split_axis=1, conc...]
    psum x1 -> x2, waiting for transfers between devices: 63.9 us -> 71.5 us  [the longest x1 71.5 us: body(): psum(low_part.astype(jnp.bfloat16), axis_name='tensor')]
    all_to_all x1, blocking collectives: 24.5 us -> 28.5 us  [body(): lax.all_to_all(b_send, 'dp', split_axis=0, concat_axis=1, tiled=True)]
  transfers between devices with their start and end apart: 5 -> 6, of which waited for: 4 -> 5; matrix products, arithmetic and copies ran while one was open for 5% -> 6% of each run, Pallas kernels for 0% -> 0%
where the time goes in v1:
time: 339 us; the launch traced here: 338 us
  waiting for transfers between devices  179 us (53%)
  blocking collectives  97.4 us (29%)
  starting transfers between devices  18.4 us (5%)
  between operations  15.8 us (5%)
  matrix products  15.1 us (4%)
  local copies, waits for them, and re-layouts  10.2 us (3%)
    psum x1, waiting for transfers between devices, body(): psum(low_part.astype(jnp.bfloat16), axis_name='tensor')  71.5 us
    all_gather x1, waiting for transfers between devices, body(): lax.all_gather(cotangent, ('pipe', 'tensor'), axis=0, tiled=True)  62.2 us
    all_to_all x1, blocking collectives, body(): lax.all_to_all(a_send, 'dp', split_axis=0, concat_axis=1, tiled=True)  44.1 us
    all_to_all x1, blocking collectives, body(): lax.all_to_all(b_send, 'dp', split_axis=0, concat_axis=1, tiled=True)  28.5 us
    all_to_all x1, waiting for transfers between devices, body(): lax.all_to_all(grad_a_part.astype(jnp.bfloat16), 'dp', split_axis=1, conc...  26.6 us
    all_gather x1, blocking collectives, body(): lax.all_gather(grad_rows, ('pipe', 'tensor'), axis=0, tiled=True)  24.8 us
    all_to_all x1, starting transfers between devices, body(): lax.all_to_all(grad_b_part.astype(jnp.bfloat16), 'dp', split_axis=1, conc...  12.3 us
    reduce_scatter x1, waiting for transfers between devices, body(): lax.psum_scatter(jnp.dot(tokens, key_value_weight, preferred_element_type...  9.04 us
  transfers between devices with their start and end apart: 6, of which 5 were waited for; matrix products, arithmetic and copies ran while one was open for 6% of the time, Pallas kernels for 0%

profile of v1, /device:TPU:2, one launch (start us, length us, event | category | flops | bytes accessed | tf_op | source)
XLA Modules:
  0.0 338.3 jit_solution(2610249351681543796)
XLA Ops:
  8.1 0.9 select_reduce_fusion
  9.0 1.3 fusion.2
  10.4 44.1 %all_to_all.57 = bf16[128,16,128]{2,1,0:T(8,128)(2,1)S(1)} all-to-all(bf16[128,16,128]{2,1,0:T(8,128)(2,1)S(1)} %bitcast.78), channel_id=1, replica_groups=mesh['dp'=16,'pipe'=4,'tensor'=8] {'dp'}, dimensions={0} | all-to-all | bytes 1048576 | tf_op jit(solution)/shard_map/all_to_all | solution.py:50
  55.6 0.9 copy.41
  56.5 71.5 %all-reduce.3.cloned.1.call-done = bf16[1024,128]{0,1:T(8,128)(2,1)} async-done(((bf16[1024,128]{0,1:T(8,128)(2,1)}), bf16[1024,128]{0,1:T(8,128)(2,1)}) %all-reduce.3.cloned.1.call-update) | async-done | bytes 262160 | tf_op jit(solution)/shard_map/psum | solution.py:58
  128.1 3.2 convolution_convert_fusion.1
  132.1 2.4 copy.61
  135.3 28.5 %all_to_all.58 = bf16[16,4,2048]{2,1,0:T(4,128)(2,1)S(1)} all-to-all(bf16[16,4,2048]{2,1,0:T(4,128)(2,1)S(1)} %reshape.64), channel_id=1, replica_groups=mesh['dp'=16,'pipe'=4,'tensor'=8] {'dp'}, dimensions={0} | all-to-all | bytes 524288 | tf_op jit(solution)/shard_map/all_to_all | solution.py:51
  164.7 24.8 %all_gather.7 = bf16[1024,128]{1,0:T(8,128)(2,1)S(1)} all-gather(bf16[32,128]{1,0:T(8,128)(2,1)S(1)} %pad_maximum_fusion), channel_id=1, replica_groups=mesh['dp'=16,'pipe'=4,'tensor'=8] {'pipe','tensor'}, dimensions={0}, use_global_device_ids=true | all-gather | bytes 270336 | tf_op jit(solution)/shard_map/all_gather | solution.py:99
  189.9 1.1 copy.43
  191.0 6.0 %all-to-all-start.2 = ((bf16[8,256,128]{2,0,1:T(8,128)(2,1)}), bf16[8,256,128]{2,0,1:T(8,128)(2,1)S(1)}, u32[]{:S(2)}, u32[]{:S(2)}) async-start(bf16[8,256,128]{2,0,1:T(8,128)(2,1)} %copy.43), calls=%async_computation.3 | async-start | bytes 1048576 | tf_op jit(solution)/shard_map/all_to_all | solution.py:123
  197.3 1.2 fusion.14
  198.5 1.2 fusion.11
  199.7 26.6 %all-to-all-done.2 = bf16[8,256,128]{2,0,1:T(8,128)(2,1)S(1)} async-done(((bf16[8,256,128]{2,0,1:T(8,128)(2,1)}), bf16[8,256,128]{2,0,1:T(8,128)(2,1)S(1)}, u32[]{:S(2)}, u32[]{:S(2)}) %all-to-all-start.2) | async-done | bytes 524320 | tf_op jit(solution)/shard_map/all_to_all | solution.py:123
  226.9 1.3 copy.53
  228.2 9.0 %reduce-scatter.2.cloned.1.call-done = bf16[32,2048]{1,0:T(8,128)(2,1)} async-done(((bf16[1024,2048]{1,0:T(8,128)(2,1)}), bf16[32,2048]{1,0:T(8,128)(2,1)}) %reduce-scatter.2.cloned.1.call-update) | async-done | bytes 131088 | tf_op jit(solution)/shard_map/reduce_scatter | solution.py:59
  237.2 1.6 fusion.7
  238.8 62.2 %all-gather.2.cloned.1.call-done = bf16[1024,2048]{1,0:T(8,128)(2,1)} async-done(((bf16[32,2048]{1,0:T(8,128)(2,1)}), bf16[1024,2048]{1,0:T(8,128)(2,1)}) %all-gather.2.cloned.1.call-update) | async-done | bytes 4194320 | tf_op jit(solution)/shard_map/all_gather | solution.py:98
  301.1 1.1 constant_dynamic-slice_fusion
  302.1 1.1 convolution_convert_fusion.5
  304.1 12.3 %all-to-all-start.3 = ((bf16[16,2,1024]{2,1,0:T(2,128)(2,1)}), bf16[16,2,1024]{2,1,0:T(2,128)(2,1)S(1)}, u32[]{:S(2)}, u32[]{:S(2)}) async-start(bf16[16,2,1024]{2,1,0:T(2,128)(2,1)} %reshape.73), calls=%async_computation.4 | async-start | bytes 131072 | tf_op jit(solution)/shard_map/all_to_all | solution.py:126
  316.4 4.3 %fusion = bf16[1024,256]{1,0:T(8,128)(2,1)} fusion(f32[1024,256]{1,0:T(8,128)S(1)} %bitcast.81, bf16[1024,2048]{1,0:T(8,128)(2,1)} %all-gather.2.cloned.1.call-done, bf16[256,2048]{1,0:T(8,128)(2,1)S(1)} %copy-done), kind=kOutput, calls=%fused_computation.4 | convolution fusion | flops 1074266112 | bytes 6815744 | tf_op jit(solution)/shard_map/dot_general | solution.py:102
  320.7 8.9 %all-to-all-done.3 = bf16[16,2,1024]{2,1,0:T(2,128)(2,1)S(1)} async-done(((bf16[16,2,1024]{2,1,0:T(2,128)(2,1)}), bf16[16,2,1024]{2,1,0:T(2,128)(2,1)S(1)}, u32[]{:S(2)}, u32[]{:S(2)}) %all-to-all-start.3) | async-done | bytes 65568 | tf_op jit(solution)/shard_map/all_to_all | solution.py:126
  330.1 0.8 fusion.19
  (42 shorter events, 6.2 us)
Async XLA Ops:
  8.0 120.1 %copy-start = (bf16[256,2048]{1,0:T(8,128)(2,1)S(1)}, bf16[256,2048]{1,0:T(8,128)(2,1)}, u32[]{:S(2)}) copy-start(bf16[256,2048]{1,0:T(8,128)(2,1)} %param.8) | copy-start | bytes 3145732
  8.0 47.3 %copy-start.1 = (bf16[1024,256]{1,0:T(8,128)(2,1)S(1)}, bf16[1024,256]{1,0:T(8,128)(2,1)}, u32[]{:S(2)}) copy-start(bf16[1024,256]{1,0:T(8,128)(2,1)} %param.7) | copy-start | bytes 1572868
  8.0 120.0 %all-reduce.3.cloned.1.call-start = ((), (), s32[]{:S(2)}) async-start(), calls=%async_computation.6 | async-start | bytes 524288 | tf_op jit(solution)/shard_map/psum | solution.py:58
  54.5 0.8 copy-start.2
  56.5 140.8 %all-reduce.5.cloned.1.call-start = ((), (), s32[]{:S(2)}) async-start(), calls=%async_computation.7 | async-start | bytes 524288 | tf_op jit(solution)/shard_map/psum | solution.py:58
  128.1 109.2 %reduce-scatter.2.cloned.1.call-start = ((), (), s32[]{:S(2)}) async-start(), calls=%async_computation.5 | async-start | bytes 4325376 | tf_op jit(solution)/shard_map/reduce_scatter | solution.py:59
  131.4 32.5 %copy-start.5 = (bf16[32,2048]{1,0:T(8,128)(2,1)S(1)}, bf16[32,2048]{1,0:T(8,128)(2,1)}, u32[]{:S(2)}) copy-start(bf16[32,2048]{1,0:T(8,128)(2,1)} %param.13) | copy-start | bytes 393220
  131.4 169.7 %all-gather.2.cloned.1.call-start = ((), (), s32[]{:S(2)}) async-start(), calls=%async_computation.8 | async-start | bytes 4325376 | tf_op jit(solution)/shard_map/all_gather | solution.py:98
  135.1 61.9 %copy-start.3 = (bf16[16,8,16,128]{3,2,0,1:T(8,128)(2,1)S(1)}, bf16[16,8,16,128]{3,2,0,1:T(8,128)(2,1)}, u32[]{:S(2)}) copy-start(bf16[16,8,16,128]{3,2,0,1:T(8,128)(2,1)} %copy-done.2) | copy-start | bytes 1572868
  163.9 0.7 copy-start.4
  191.0 35.3 %all-to-all-start.2 = ((bf16[8,256,128]{2,0,1:T(8,128)(2,1)}), bf16[8,256,128]{2,0,1:T(8,128)(2,1)S(1)}, u32[]{:S(2)}, u32[]{:S(2)}) async-start(bf16[8,256,128]{2,0,1:T(8,128)(2,1)} %copy.43), calls=%async_computation.3 | async-start | bytes 1048576 | tf_op jit(solution)/shard_map/all_to_all | solution.py:123
  304.1 25.5 %all-to-all-start.3 = ((bf16[16,2,1024]{2,1,0:T(2,128)(2,1)}), bf16[16,2,1024]{2,1,0:T(2,128)(2,1)S(1)}, u32[]{:S(2)}, u32[]{:S(2)}) async-start(bf16[16,2,1024]{2,1,0:T(2,128)(2,1)} %reshape.73), calls=%async_computation.4 | async-start | bytes 131072 | tf_op jit(solution)/shard_map/all_to_all | solution.py:126
Sparse Core Ops, SparseCore 0:
  56.6 71.3 all-reduce.2
  130.3 55.4 all-reduce.4
Sparse Core Ops, SparseCore 1:
  133.0 104.1 reduce-scatter.1
  240.3 60.7 all-gather.1
